TPU v7x, 256 devices: a whole 4x4x8 slice. The times are simulated.
256 devices in a mesh: expert: 32 (over z, y), etp: 8 (over x, core).
Axes of the slice: x: 4, y: 4, z: 8, core: 2. Of those that a mesh axis runs over, the one named last changes fastest.
Arguments:
- tokens: bfloat16 [32768, 2560], P(('expert', 'etp')), may hold values from -6 to 6
- grad_out: bfloat16 [32768, 2560], P(('expert', 'etp')), may hold values from -6 to 6
- router_weight: bfloat16 [2560, 32], replicated, may hold values from -0.125 to 0.125
- expert_choice: int32 [32768, 1], P(('expert', 'etp')), may hold values from 0 to 31; in each aligned block of 128 rows (0 to 127, 128 to 255, ...) at most 6 rows name the same one
- gate_pre: bfloat16 [32, 1536, 4096], P('expert', None, 'etp'), may hold values from -6 to 6
- up_pre: bfloat16 [32, 1536, 4096], P('expert', None, 'etp'), may hold values from -6 to 6
- w_gate: bfloat16 [32, 2560, 4096], P('expert', None, 'etp'), may hold values from -0.125 to 0.125
- w_up: bfloat16 [32, 2560, 4096], P('expert', None, 'etp'), may hold values from -0.125 to 0.125
- w_down: bfloat16 [32, 4096, 2560], P('expert', 'etp'), may hold values from -0.09375 to 0.09375
Outputs:
- token_grad: bfloat16 [32768, 2560], P(('expert', 'etp'))
- router_grad: float32 [2560, 32], replicated
Inputs may be any that keep to these rules, and one draw needn't show every extreme that they name: `expert_choice`: within the 128 tokens of one device no expert is chosen more than 6 times, and in every draw some expert is chosen exactly 6 times by the tokens of some device.
All inputs are finite; a program needn't handle non-finite values.
Results may differ from a plain program's by a relative error of at most 0.015.
Values may be sent and summed in bfloat16 or wider, within the bound.
No kernel may reach another device: no remote copies, remote signals or barrier semaphores. Data moves between devices by JAX's collectives and lax.ppermute only.
A program may use at most 128 MiB of HBM per device.

v0:
```python
import jax
import jax.numpy as jnp
from jax import lax
from jax.sharding import PartitionSpec as P


def local(tokens, grad_out, router_weight, expert_choice, gate_pre, up_pre, w_gate, w_up, w_down):
    width = tokens.shape[1]
    experts = router_weight.shape[1]
    n_expert = lax.axis_size("expert")
    n_etp = lax.axis_size("etp")
    capacity = gate_pre.shape[1] // (n_expert * n_etp)
    hidden = w_down.shape[1]
    contract = (((1,), (1,)), ((), ()))
    chosen_ids = expert_choice[:, 0]
    picked = chosen_ids[:, None] == jnp.arange(experts, dtype=jnp.int32)[None, :]
    logits = jnp.dot(tokens, router_weight, preferred_element_type=jnp.float32)
    score = jax.nn.sigmoid(jnp.sum(jnp.where(picked, logits, 0.0), axis=1))
    counts = picked.astype(jnp.int32)
    earlier = jnp.cumsum(counts, axis=0) - counts
    position = jnp.sum(earlier * counts, axis=1)
    target = chosen_ids * capacity + position
    outgoing = jnp.zeros((experts * capacity, width), jnp.bfloat16).at[target].set(grad_out)
    gate_all = gate_pre[0]
    up_all = up_pre[0]
    gate_w = w_gate[0]
    up_w = w_up[0]
    down_w = w_down[0]
    pooled = lax.all_gather(outgoing, "etp", axis=0, tiled=True)
    pooled = pooled.reshape(n_etp, experts * capacity, width)
    arrived = lax.all_to_all(pooled, "expert", split_axis=1, concat_axis=1, tiled=True)
    d_hidden = lax.dot_general(
        arrived.reshape(n_etp * experts * capacity, width),
        down_w,
        contract,
        preferred_element_type=jnp.float32,
    )
    gate_f = gate_all.astype(jnp.float32)
    up_f = up_all.astype(jnp.float32)
    sig = jax.nn.sigmoid(gate_f)
    d_gate = (d_hidden * up_f * sig * (1.0 + gate_f * (1.0 - sig))).astype(jnp.bfloat16)
    d_up = (d_hidden * gate_f * sig).astype(jnp.bfloat16)
    both = jnp.concatenate([d_gate, d_up], axis=1)
    term = lax.dot_general(both[:, :hidden], gate_w, contract, preferred_element_type=jnp.float32)
    terms = (
        term + lax.dot_general(both[:, hidden:], up_w, contract, preferred_element_type=jnp.float32)
    ).astype(jnp.bfloat16)
    terms = terms.reshape(n_etp, experts * capacity, width)
    swapped = lax.all_to_all(terms, "expert", split_axis=1, concat_axis=1, tiled=True)
    summed = lax.psum_scatter(swapped, "etp", scatter_dimension=0, tiled=True).astype(jnp.float32)
    returned = summed.reshape(experts * capacity, width).astype(jnp.bfloat16)
    fetched = returned[target].astype(jnp.float32)
    inputs = tokens.astype(jnp.float32)
    d_logit = jnp.sum(inputs * fetched, axis=1) * score * (1.0 - score)
    column = lax.dot_general(
        picked.astype(jnp.bfloat16), router_weight, contract, preferred_element_type=jnp.float32
    )
    token_grad = (score[:, None] * fetched + d_logit[:, None] * column).astype(jnp.bfloat16)
    weighted = jnp.where(picked, d_logit[:, None], 0.0)
    local_terms = jnp.dot(
        inputs.T, weighted, precision=lax.Precision.HIGHEST, preferred_element_type=jnp.float32
    )
    router_grad = lax.psum(local_terms, ("expert", "etp"))
    return (token_grad, router_grad)


def solution(mesh):
    placed = (
        P(("expert", "etp"), None),
        P(("expert", "etp"), None),
        P(),
        P(("expert", "etp"), None),
        P("expert", None, "etp"),
        P("expert", None, "etp"),
        P("expert", None, "etp"),
        P("expert", None, "etp"),
        P("expert", "etp", None),
    )
    return jax.shard_map(
        local,
        mesh=mesh,
        in_specs=placed,
        out_specs=(P(("expert", "etp"), None), P()),
        check_vma=False,
    )
```

profile of v0, /device:TPU:1, one launch (start us, length us, event | category | flops | bytes accessed | tf_op | source)
XLA Modules:
  0.0 812.3 jit_solution(2076231841087327123)
XLA Ops:
  7.2 0.8 fusion.28
  8.4 0.7 select_reduce_fusion
  9.1 0.7 fusion.33
  9.7 3.2 scatter_custom_fusion
  13.0 54.4 %all-gather.2.cloned.1.call-done = bf16[1536,2560]{1,0:T(8,128)(2,1)} async-done(((bf16[192,2560]{1,0:T(8,128)(2,1)}), bf16[1536,2560]{1,0:T(8,128)(2,1)}) %all-gather.2.cloned.1.call-update) | async-done | bytes 7864336 | tf_op jit(solution)/shard_map/all_gather | solution.py:29
  67.4 10.7 %copy.22 = bf16[8,192,2560]{2,0,1:T(8,128)(2,1)} copy(bf16[8,192,2560]{2,1,0:T(8,128)(2,1)} %bitcast.44) | data formatting | bytes 15728640 | tf_op jit(solution)/shard_map/reshape | solution.py:30
  78.1 183.8 %all_to_all.10 = bf16[8,192,2560]{2,0,1:T(8,128)(2,1)} all-to-all(bf16[8,192,2560]{2,0,1:T(8,128)(2,1)} %copy.22), channel_id=1, replica_groups=mesh['expert'=32,'etp'=8] {'expert'}, dimensions={1} | all-to-all | bytes 15728640 | tf_op jit(solution)/shard_map/all_to_all | solution.py:31
  261.9 9.0 %copy.23 = bf16[8,192,2560]{2,1,0:T(8,128)(2,1)} copy(bf16[8,192,2560]{2,0,1:T(8,128)(2,1)} %all_to_all.10) | data formatting | bytes 15728640 | tf_op jit(solution)/shard_map/all_to_all | solution.py:31
  270.8 6.7 fusion.14
  277.6 1.7 copy-done.8
  279.3 9.9 %fusion.12 = f32[1536,2560]{1,0:T(8,128)} fusion(bf16[1,2560,512]{2,1,0:T(8,128)(2,1)S(1)} %copy-done, f32[1536,512]{1,0:T(8,128)S(1)} %fusion.14, bf16[1,1536,512]{2,1,0:T(8,128)(2,1)S(1)} %copy-done.6, bf16[1,1536,512]{2,1,0:T(8,128)(2,1)S(1)} %copy-done.7), kind=kOutput, calls=%fused_computation.21 | convolution fusion | flops 4035969024 | bytes 24641536 | tf_op jit(solution)/shard_map/dot_general | solution.py:44
  289.2 15.2 %add_convert_fusion = bf16[1536,2560]{1,0:T(8,128)(2,1)} fusion(f32[1536,2560]{1,0:T(8,128)} %fusion.12, bf16[1,2560,512]{2,1,0:T(8,128)(2,1)} %param.16, f32[1536,512]{1,0:T(8,128)} %copy-done.8, bf16[1,1536,512]{2,1,0:T(8,128)(2,1)} %param.13), kind=kOutput, calls=%fused_computation.2 | convolution fusion | flops 4039901184 | bytes 30932992 | tf_op jit(solution)/shard_map/dot_general | solution.py:46
  304.5 10.6 %copy.24 = bf16[8,192,2560]{2,0,1:T(8,128)(2,1)} copy(bf16[8,192,2560]{2,1,0:T(8,128)(2,1)} %bitcast.45) | data formatting | bytes 15728640 | tf_op jit(solution)/shard_map/reshape | solution.py:48
  315.1 177.6 %all_to_all.11 = bf16[8,192,2560]{2,0,1:T(8,128)(2,1)} all-to-all(bf16[8,192,2560]{2,0,1:T(8,128)(2,1)} %copy.24), channel_id=1, replica_groups=mesh['expert'=32,'etp'=8] {'expert'}, dimensions={1} | all-to-all | bytes 15728640 | tf_op jit(solution)/shard_map/all_to_all | solution.py:49
  492.6 8.7 %copy.25 = bf16[8,192,2560]{2,1,0:T(8,128)(2,1)} copy(bf16[8,192,2560]{2,0,1:T(8,128)(2,1)} %all_to_all.11) | data formatting | bytes 15728640 | tf_op jit(solution)/shard_map/all_to_all | solution.py:49
  501.5 1.0 copy-done.2
  502.5 0.3 fusion.24
  502.8 48.4 %reduce-scatter.2.cloned.1.call-done = bf16[1,192,2560]{2,1,0:T(8,128)(2,1)} async-done(((bf16[8,192,2560]{2,1,0:T(8,128)(2,1)}), bf16[1,192,2560]{2,1,0:T(8,128)(2,1)}) %reduce-scatter.2.cloned.1.call-update) | async-done | bytes 983056 | tf_op jit(solution)/shard_map/reduce_scatter | solution.py:50
  551.2 3.9 gather_fusion
  555.2 1.3 fusion.23
  556.5 1.1 convolution_bitcast_fusion
  557.7 2.3 fusion.1
  560.0 244.0 %all-reduce.2.cloned.1.call-done = f32[2560,32]{0,1:T(8,128)} async-done(((f32[2560,32]{0,1:T(8,128)}), f32[2560,32]{0,1:T(8,128)}) %all-reduce.2.cloned.1.call-update) | async-done | bytes 327696 | tf_op jit(solution)/shard_map/psum | solution.py:63
  804.0 1.7 copy.27
  (27 shorter events, 0.6 us)
Async XLA Ops:
  7.2 272.1 %copy-start = (bf16[1,2560,512]{2,1,0:T(8,128)(2,1)S(1)}, bf16[1,2560,512]{2,1,0:T(8,128)(2,1)}, u32[]{:S(2)}) copy-start(bf16[1,2560,512]{2,1,0:T(8,128)(2,1)} %param.15) | copy-start | bytes 7864324
  7.2 60.2 %all-gather.2.cloned.1.call-start = ((), (), s32[]{:S(2)}) async-start(), calls=%async_computation.3 | async-start | bytes 8847360 | tf_op jit(solution)/shard_map/all_gather | solution.py:29
  13.0 538.3 %reduce-scatter.2.cloned.1.call-start = ((), (), s32[]{:S(2)}) async-start(), calls=%async_computation.4 | async-start | bytes 8847360 | tf_op jit(solution)/shard_map/reduce_scatter | solution.py:50
  261.9 9.0 %copy-start.5 = (bf16[1,512,2560]{2,1,0:T(8,128)(2,1)S(1)}, bf16[1,512,2560]{2,1,0:T(8,128)(2,1)}, u32[]{:S(2)}) copy-start(bf16[1,512,2560]{2,1,0:T(8,128)(2,1)} %param.17) | copy-start | bytes 7864324
  270.8 8.5 %copy-start.6 = (bf16[1,1536,512]{2,1,0:T(8,128)(2,1)S(1)}, bf16[1,1536,512]{2,1,0:T(8,128)(2,1)}, u32[]{:S(2)}) copy-start(bf16[1,1536,512]{2,1,0:T(8,128)(2,1)} %param.14) | copy-start | bytes 4718596
  270.8 8.5 %copy-start.7 = (bf16[1,1536,512]{2,1,0:T(8,128)(2,1)S(1)}, bf16[1,1536,512]{2,1,0:T(8,128)(2,1)}, u32[]{:S(2)}) copy-start(bf16[1,1536,512]{2,1,0:T(8,128)(2,1)} %param.13) | copy-start | bytes 4718596
  277.6 1.7 copy-start.8
  501.4 1.1 copy-start.2
  501.4 1.1 copy-start.3
  501.4 1.1 copy-start.4
  501.4 302.6 %all-reduce.2.cloned.1.call-start = ((), (), s32[]{:S(2)}) async-start(), calls=%async_computation.5 | async-start | bytes 655360 | tf_op jit(solution)/shard_map/psum | solution.py:63
  551.2 254.5 %copy-start.1 = (bf16[1,2560,512]{2,1,0:T(8,128)(2,1)S(1)}, bf16[1,2560,512]{2,1,0:T(8,128)(2,1)}, u32[]{:S(2)}) copy-start(bf16[1,2560,512]{2,1,0:T(8,128)(2,1)} %param.15) | copy-start | bytes 7864324
Sparse Core Ops, SparseCore 0:
  13.1 54.2 all-gather.1
  501.5 49.6 reduce-scatter.1
  557.8 246.1 all-reduce.1
where the time goes:
time: 813 us; the launch traced here: 812 us
  blocking collectives  361 us (44%)
  waiting for transfers between devices  347 us (43%)
  local copies, waits for them, and re-layouts  50.8 us (6%)
  matrix products  35.6 us (4%)
  between operations  13.8 us (2%)
    psum x1, waiting for transfers between devices, local(): router_grad = lax.psum(local_terms, ('expert', 'etp'))  244 us
    all_to_all x1, blocking collectives, local(): lax.all_to_all(pooled, 'expert', split_axis=1, concat_axis=1, tiled=True)  184 us
    all_to_all x1, blocking collectives, local(): lax.all_to_all(terms, 'expert', split_axis=1, concat_axis=1, tiled=True)  178 us
    all_gather x1, waiting for transfers between devices, local(): pooled = lax.all_gather(outgoing, 'etp', axis=0, tiled=True)  54.4 us
    reduce_scatter x1, waiting for transfers between devices, local(): lax.psum_scatter(swapped, 'etp', scatter_dimension=0, tiled=True)  48.4 us
  transfers between devices with their start and end apart: 3, of which 3 were waited for; matrix products, arithmetic and copies ran while one was open for 0% of the time, Pallas kernels for 0%

commit v1 on v0

--- a/solution.py
+++ b/solution.py
@@ -2,6 +2,27 @@
 import jax.numpy as jnp
 from jax import lax
 from jax.sharding import PartitionSpec as P
+
+
+def collect(x, axis, dim):
+    size, position, rows = (lax.axis_size(axis), lax.axis_index(axis), x.shape[dim])
+    ahead = [(i, (i + 1) % size) for i in range(size)]
+    backward = [(i, (i - 1) % size) for i in range(size)]
+    filled = jnp.zeros((*x.shape[:dim], size * rows, *x.shape[dim + 1 :]), x.dtype)
+    filled = lax.dynamic_update_slice_in_dim(filled, x, position * rows, axis=dim)
+    from_left = from_right = x
+    halfway = size // 2
+    for lap in range(1, halfway + 1):
+        from_left = lax.ppermute(from_left, axis, ahead)
+        filled = lax.dynamic_update_slice_in_dim(
+            filled, from_left, (position - lap) % size * rows, axis=dim
+        )
+        if lap < size - halfway:
+            from_right = lax.ppermute(from_right, axis, backward)
+            filled = lax.dynamic_update_slice_in_dim(
+                filled, from_right, (position + lap) % size * rows, axis=dim
+            )
+    return filled
 
 
 def local(tokens, grad_out, router_weight, expert_choice, gate_pre, up_pre, w_gate, w_up, w_down):
@@ -26,7 +47,7 @@
     gate_w = w_gate[0]
     up_w = w_up[0]
     down_w = w_down[0]
-    pooled = lax.all_gather(outgoing, "etp", axis=0, tiled=True)
+    pooled = collect(outgoing, "etp", 0)
     pooled = pooled.reshape(n_etp, experts * capacity, width)
     arrived = lax.all_to_all(pooled, "expert", split_axis=1, concat_axis=1, tiled=True)
     d_hidden = lax.dot_general(

time: 813 us -> 820 us (level)
  local copies, waits for them, and re-layouts: 50.8 us -> 66.1 us
  starting transfers between devices: 0.12 us -> 15.3 us
  waiting for transfers between devices: 347 us -> 332 us
  blocking collectives: 361 us -> 352 us
    all_gather x1 -> x0, waiting for transfers between devices: 54.4 us -> none  [local(): pooled = lax.all_gather(outgoing, 'etp', axis=0, tiled=True)]
    ppermute x0 -> x7, waiting for transfers between devices: none -> 25.4 us  [the longest x4 23 us: collect(): from_left = lax.ppermute(from_left, axis, ahead)]
    ppermute x0 -> x7, starting transfers between devices: none -> 15.2 us  [the longest x4 9.94 us: collect(): from_left = lax.ppermute(from_left, axis, ahead)]
    reduce_scatter x1, waiting for transfers between devices: 48.4 us -> 62.9 us  [local(): lax.psum_scatter(swapped, 'etp', scatter_dimension=0, tiled=True)]
    dynamic_update_slice x0 -> x8, local copies, waits for them, and re-layouts: none -> 11.8 us  [the longest x4 6.52 us: collect(): lax.dynamic_update_slice_in_dim(filled, from_left, (position - lap) % siz...]
  transfers between devices with their start and end apart: 3 -> 9, of which waited for: 3 -> 8; matrix products, arithmetic and copies ran while one was open for 0% -> 2% of each run, Pallas kernels for 0% -> 0%
where the time goes in v1:
time: 820 us; the launch traced here: 819 us
  blocking collectives  352 us (43%)
  waiting for transfers between devices  332 us (40%)
  local copies, waits for them, and re-layouts  66.1 us (8%)
  matrix products  35.7 us (4%)
  starting transfers between devices  15.3 us (2%)
  between operations  14.1 us (2%)
    psum x1, waiting for transfers between devices, local(): router_grad = lax.psum(local_terms, ('expert', 'etp'))  244 us
    all_to_all x1, blocking collectives, local(): lax.all_to_all(pooled, 'expert', split_axis=1, concat_axis=1, tiled=True)  179 us
    all_to_all x1, blocking collectives, local(): lax.all_to_all(terms, 'expert', split_axis=1, concat_axis=1, tiled=True)  173 us
    reduce_scatter x1, waiting for transfers between devices, local(): lax.psum_scatter(swapped, 'etp', scatter_dimension=0, tiled=True)  62.9 us
    ppermute x4, waiting for transfers between devices, collect(): from_left = lax.ppermute(from_left, axis, ahead)  23 us
  transfers between devices with their start and end apart: 9, of which 8 were waited for; matrix products, arithmetic and copies ran while one was open for 2% of the time, Pallas kernels for 0%

profile of v1, /device:TPU:1, one launch (start us, length us, event | category | flops | bytes accessed | tf_op | source)
XLA Modules:
  0.0 819.4 jit_solution(1929266241360226068)
XLA Ops:
  9.7 3.1 scatter_custom_fusion
  12.8 2.6 collective-permute-start
  16.1 10.7 %collective-permute-done = bf16[192,2560]{1,0:T(8,128)(2,1)} collective-permute-done((bf16[192,2560]{1,0:T(8,128)(2,1)}, bf16[192,2560]{1,0:T(8,128)(2,1)}, u32[]{:S(2)}, u32[]{:S(2)}) %collective-permute-start) | collective-permute-done | bytes 983072 | tf_op jit(solution)/shard_map/ppermute | solution.py:16
  26.8 2.5 collective-permute-start.2
  31.2 3.6 broadcast_in_dim.27
  35.8 4.8 collective-permute-done.2
  40.6 2.5 collective-permute-start.4
  43.1 2.2 constant_dynamic-update-slice_fusion.5
  47.6 3.1 collective-permute-start.5
  54.5 2.4 collective-permute-start.6
  62.1 5.8 collective-permute-done.6
  68.9 10.7 %copy.21 = bf16[8,192,2560]{2,0,1:T(8,128)(2,1)} copy(bf16[8,192,2560]{2,1,0:T(8,128)(2,1)} %bitcast.3) | data formatting | bytes 15728640 | tf_op jit(solution)/shard_map/reshape | solution.py:51
  79.6 178.7 %all_to_all.10 = bf16[8,192,2560]{2,0,1:T(8,128)(2,1)} all-to-all(bf16[8,192,2560]{2,0,1:T(8,128)(2,1)} %copy.21), channel_id=1, replica_groups=mesh['expert'=32,'etp'=8] {'expert'}, dimensions={1} | all-to-all | bytes 15728640 | tf_op jit(solution)/shard_map/all_to_all | solution.py:52
  258.3 9.0 %copy.22 = bf16[8,192,2560]{2,1,0:T(8,128)(2,1)} copy(bf16[8,192,2560]{2,0,1:T(8,128)(2,1)} %all_to_all.10) | data formatting | bytes 15728640 | tf_op jit(solution)/shard_map/all_to_all | solution.py:52
  267.3 6.7 fusion.14
  275.8 9.9 %fusion.12 = f32[1536,2560]{1,0:T(8,128)} fusion(bf16[1,2560,512]{2,1,0:T(8,128)(2,1)S(1)} %copy-done, f32[1536,512]{1,0:T(8,128)S(1)} %fusion.14, bf16[1,1536,512]{2,1,0:T(8,128)(2,1)S(1)} %copy-done.7, bf16[1,1536,512]{2,1,0:T(8,128)(2,1)S(1)} %copy-done.8), kind=kOutput, calls=%fused_computation.21 | convolution fusion | flops 4035969024 | bytes 24641536 | tf_op jit(solution)/shard_map/dot_general | solution.py:65
  285.7 15.3 %add_convert_fusion = bf16[1536,2560]{1,0:T(8,128)(2,1)} fusion(f32[1536,2560]{1,0:T(8,128)} %fusion.12, bf16[1,2560,512]{2,1,0:T(8,128)(2,1)} %param.16, f32[1536,512]{1,0:T(8,128)} %copy-done.9, bf16[1,1536,512]{2,1,0:T(8,128)(2,1)} %param.13), kind=kOutput, calls=%fused_computation.2 | convolution fusion | flops 4039901184 | bytes 30932992 | tf_op jit(solution)/shard_map/dot_general | solution.py:67
  301.0 10.6 %copy.23 = bf16[8,192,2560]{2,0,1:T(8,128)(2,1)} copy(bf16[8,192,2560]{2,1,0:T(8,128)(2,1)} %bitcast.44) | data formatting | bytes 15728640 | tf_op jit(solution)/shard_map/reshape | solution.py:69
  311.6 173.5 %all_to_all.11 = bf16[8,192,2560]{2,0,1:T(8,128)(2,1)} all-to-all(bf16[8,192,2560]{2,0,1:T(8,128)(2,1)} %copy.23), channel_id=1, replica_groups=mesh['expert'=32,'etp'=8] {'expert'}, dimensions={1} | all-to-all | bytes 15728640 | tf_op jit(solution)/shard_map/all_to_all | solution.py:70
  485.0 8.7 %copy.24 = bf16[8,192,2560]{2,1,0:T(8,128)(2,1)} copy(bf16[8,192,2560]{2,0,1:T(8,128)(2,1)} %all_to_all.11) | data formatting | bytes 15728640 | tf_op jit(solution)/shard_map/all_to_all | solution.py:70
  495.2 62.9 %reduce-scatter.2.cloned.1.call-done = bf16[1,192,2560]{2,1,0:T(8,128)(2,1)} async-done(((bf16[8,192,2560]{2,1,0:T(8,128)(2,1)}), bf16[1,192,2560]{2,1,0:T(8,128)(2,1)}) %reduce-scatter.2.cloned.1.call-update) | async-done | bytes 983056 | tf_op jit(solution)/shard_map/reduce_scatter | solution.py:71
  558.1 3.9 gather_fusion
  564.5 2.3 fusion.1
  566.8 244.0 %all-reduce.2.cloned.1.call-done = f32[2560,32]{0,1:T(8,128)} async-done(((f32[2560,32]{0,1:T(8,128)}), f32[2560,32]{0,1:T(8,128)}) %all-reduce.2.cloned.1.call-update) | async-done | bytes 327696 | tf_op jit(solution)/shard_map/psum | solution.py:84
  (49 shorter events, 25.8 us)
Async XLA Ops:
  7.2 268.6 %copy-start = (bf16[1,2560,512]{2,1,0:T(8,128)(2,1)S(1)}, bf16[1,2560,512]{2,1,0:T(8,128)(2,1)}, u32[]{:S(2)}) copy-start(bf16[1,2560,512]{2,1,0:T(8,128)(2,1)} %param.15) | copy-start | bytes 7864324
  7.2 550.9 %reduce-scatter.2.cloned.1.call-start = ((), (), s32[]{:S(2)}) async-start(), calls=%async_computation.3 | async-start | bytes 8847360 | tf_op jit(solution)/shard_map/reduce_scatter | solution.py:71
  12.8 14.0 %collective-permute-start = (bf16[192,2560]{1,0:T(8,128)(2,1)}, bf16[192,2560]{1,0:T(8,128)(2,1)}, u32[]{:S(2)}, u32[]{:S(2)}) collective-permute-start(bf16[192,2560]{1,0:T(8,128)(2,1)} %scatter_custom_fusion), channel_id=1, source_target_pairs={{0,1},{1,2},{2,3},{3,4},{4,5},{5,6},{6,7},{7,0},{8,9},{9,10},{10,1... | collective-permute-start | bytes 2949128 | tf_op jit(solution)/shard_map/ppermute | solution.py:16
  15.4 14.1 %collective-permute-start.1 = (bf16[192,2560]{1,0:T(8,128)(2,1)}, bf16[192,2560]{1,0:T(8,128)(2,1)}, u32[]{:S(2)}, u32[]{:S(2)}) collective-permute-start(bf16[192,2560]{1,0:T(8,128)(2,1)} %scatter_custom_fusion), channel_id=1, source_target_pairs={{0,7},{1,0},{2,1},{3,2},{4,3},{5,4},{6,5},{7,6},{8,15},{9,8},{10,9... | collective-permute-start | bytes 2949128 | tf_op jit(solution)/shard_map/ppermute | solution.py:21
  26.8 13.8 %collective-permute-start.2 = (bf16[192,2560]{1,0:T(8,128)(2,1)}, bf16[192,2560]{1,0:T(8,128)(2,1)}, u32[]{:S(2)}, u32[]{:S(2)}) collective-permute-start(bf16[192,2560]{1,0:T(8,128)(2,1)} %collective-permute-done), channel_id=1, source_target_pairs={{0,1},{1,2},{2,3},{3,4},{4,5},{5,6},{6,7},{7,0},{8,9},{9,10},{10,1... | collective-permute-start | bytes 2949128 | tf_op jit(solution)/shard_map/ppermute | solution.py:16
  29.3 5.5 copy-start.3
  29.6 18.0 %collective-permute-start.3 = (bf16[192,2560]{1,0:T(8,128)(2,1)}, bf16[192,2560]{1,0:T(8,128)(2,1)S(1)}, u32[]{:S(2)}, u32[]{:S(2)}) collective-permute-start(bf16[192,2560]{1,0:T(8,128)(2,1)} %collective-permute-done.1), channel_id=1, source_target_pairs={{0,7},{1,0},{2,1},{3,2},{4,3},{5,4},{6,5},{7,6},{8,15},{9,8},{10,9... | collective-permute-start | bytes 2949128 | tf_op jit(solution)/shard_map/ppermute | solution.py:21
  40.6 13.8 %collective-permute-start.4 = (bf16[192,2560]{1,0:T(8,128)(2,1)}, bf16[192,2560]{1,0:T(8,128)(2,1)S(1)}, u32[]{:S(2)}, u32[]{:S(2)}) collective-permute-start(bf16[192,2560]{1,0:T(8,128)(2,1)} %collective-permute-done.2), channel_id=1, source_target_pairs={{0,1},{1,2},{2,3},{3,4},{4,5},{5,6},{6,7},{7,0},{8,9},{9,10},{10,1... | collective-permute-start | bytes 2949128 | tf_op jit(solution)/shard_map/ppermute | solution.py:16
  47.6 13.5 %collective-permute-start.5 = (bf16[192,2560]{1,0:T(8,128)(2,1)S(1)}, bf16[192,2560]{1,0:T(8,128)(2,1)S(1)}, u32[]{:S(2)}, u32[]{:S(2)}) collective-permute-start(bf16[192,2560]{1,0:T(8,128)(2,1)S(1)} %collective-permute-done.3), channel_id=1, source_target_pairs={{0,7},{1,0},{2,1},{3,2},{4,3},{5,4},{6,5},{7,6},{8,15},{9,8},{10,9... | collective-permute-start | bytes 2949128 | tf_op jit(solution)/shard_map/ppermute | solution.py:21
  54.5 13.4 %collective-permute-start.6 = (bf16[192,2560]{1,0:T(8,128)(2,1)S(1)}, bf16[192,2560]{1,0:T(8,128)(2,1)S(1)}, u32[]{:S(2)}, u32[]{:S(2)}) collective-permute-start(bf16[192,2560]{1,0:T(8,128)(2,1)S(1)} %collective-permute-done.4), channel_id=1, source_target_pairs={{0,1},{1,2},{2,3},{3,4},{4,5},{5,6},{6,7},{7,0},{8,9},{9,10},{10,1... | collective-permute-start | bytes 2949128 | tf_op jit(solution)/shard_map/ppermute | solution.py:16
  258.3 9.0 %copy-start.6 = (bf16[1,512,2560]{2,1,0:T(8,128)(2,1)S(1)}, bf16[1,512,2560]{2,1,0:T(8,128)(2,1)}, u32[]{:S(2)}) copy-start(bf16[1,512,2560]{2,1,0:T(8,128)(2,1)} %param.17) | copy-start | bytes 7864324
  267.3 8.5 %copy-start.7 = (bf16[1,1536,512]{2,1,0:T(8,128)(2,1)S(1)}, bf16[1,1536,512]{2,1,0:T(8,128)(2,1)}, u32[]{:S(2)}) copy-start(bf16[1,1536,512]{2,1,0:T(8,128)(2,1)} %param.14) | copy-start | bytes 4718596
  267.3 8.5 %copy-start.8 = (bf16[1,1536,512]{2,1,0:T(8,128)(2,1)S(1)}, bf16[1,1536,512]{2,1,0:T(8,128)(2,1)}, u32[]{:S(2)}) copy-start(bf16[1,1536,512]{2,1,0:T(8,128)(2,1)} %param.13) | copy-start | bytes 4718596
  274.0 1.7 copy-start.9
  493.8 1.1 copy-start.2
  493.8 1.1 copy-start.4
  493.8 1.1 copy-start.5
  493.8 317.0 %all-reduce.2.cloned.1.call-start = ((), (), s32[]{:S(2)}) async-start(), calls=%async_computation.4 | async-start | bytes 655360 | tf_op jit(solution)/shard_map/psum | solution.py:84
  558.1 254.5 %copy-start.1 = (bf16[1,2560,512]{2,1,0:T(8,128)(2,1)S(1)}, bf16[1,2560,512]{2,1,0:T(8,128)(2,1)}, u32[]{:S(2)}) copy-start(bf16[1,2560,512]{2,1,0:T(8,128)(2,1)} %param.15) | copy-start | bytes 7864324
Sparse Core Ops, SparseCore 0:
  493.9 64.1 reduce-scatter.1
  564.7 246.1 all-reduce.1
